TPU v7x, 128 devices: a whole 4x4x4 slice. The times are simulated.
128 devices in a mesh: row: 8 (over x, core), col: 16 (over z, y).
Axes of the slice: x: 4, y: 4, z: 4, core: 2. Of those that a mesh axis runs over, the one named last changes fastest.
Arguments:
- dinv_root: bfloat16 [16384, 16384], P('row', 'col'), may hold values from -0.03125 to 0.03125
- rhs_root: bfloat16 [16384, 384], P('col'), may hold values from -6 to 6
- dinv_mid: bfloat16 [32768, 8192], P('row', 'col'), may hold values from -0.046875 to 0.046875
- coup_mid: bfloat16 [32768, 8192], P('row', 'col'), may hold values from -0.0625 to 0.0625
- rhs_mid: bfloat16 [4, 8192, 384], P(None, 'col'), may hold values from -6 to 6
- dinv_leaf: bfloat16 [16, 4096, 4096], P('col', None, 'row'), may hold values from -0.0625 to 0.0625
- coup_leaf: bfloat16 [16, 6144, 4096], P('col', 'row'), may hold values from -0.109375 to 0.109375
- rhs_leaf: bfloat16 [16, 4096, 384], P('col', 'row'), may hold values from -6 to 6
- bounds_mid: int32 [4, 64], replicated, may hold values from 0 to 127, as said below
- bounds_leaf: int32 [16, 48], replicated, may hold values from 0 to 191, as said below
- parents: int32 [16], replicated, may hold values from 0 to 3, as said below
Outputs:
- root_values: bfloat16 [16384, 384], P(('row', 'col'))
- mid_values: bfloat16 [32768, 384], P(('row', 'col'))
- leaf_values: bfloat16 [16, 4096, 384], P('col', 'row')
Inputs may be any that keep to these rules, and one draw needn't show every extreme that they name: `bounds_mid`: each row holds 64 distinct root block numbers; every root block appears in some row. `parents`: each mid front is the parent of exactly 4 leaf fronts. `bounds_leaf`: each row holds 48 distinct values. Every row names the same number of root blocks; the leaf fronts of one parent together name each block of that parent's separator exactly once, each naming 8192 / 128 / 4 of them.
All inputs are finite; a program needn't handle non-finite values.
Results may differ from a plain program's by a relative error of at most 0.0065.
Values may be sent and summed in bfloat16 or wider, within the bound.
A program may use at most 128 MiB of HBM per device.

v0:
```python
import jax
import jax.numpy as jnp
from jax import lax
from jax.sharding import PartitionSpec as P

N0 = 16384
BLOCK = 128


def partner(value, axis, distance):
    mask = 2**distance
    pairs = [(source, source ^ mask) for source in range(lax.axis_size(axis))]
    return lax.ppermute(value, axis, pairs)


def pick_blocks(shard_rows, wanted):
    block_count = shard_rows.shape[0] // BLOCK
    flat_blocks = shard_rows.reshape(block_count, BLOCK * shard_rows.shape[1])
    present = jnp.arange(block_count, dtype=jnp.int32)
    select = (wanted[:, None] == present[None, :]).astype(shard_rows.dtype)
    return jnp.dot(select, flat_blocks, preferred_element_type=jnp.float32)


def transposed_product(coupling, boundary):
    return lax.dot_general(
        coupling, boundary, (((0,), (0,)), ((), ())), preferred_element_type=jnp.float32
    )


def shards(
    dinv_root,
    rhs_root,
    dinv_mid,
    coup_mid,
    rhs_mid,
    dinv_leaf,
    coup_leaf,
    rhs_leaf,
    bounds_mid,
    bounds_leaf,
    parents,
):
    row_total = lax.axis_size("row")
    row_id = lax.axis_index("row")
    col_id = lax.axis_index("col")
    rhs_width = rhs_root.shape[1]
    root_total = N0 // BLOCK
    front_mid = row_id // 2
    half_index = row_id % 2
    half_blocks = bounds_mid.shape[1] // 2
    mid_all = lax.dynamic_slice_in_dim(bounds_mid, front_mid, 1, 0)[0]
    mid_list = lax.dynamic_slice_in_dim(mid_all, half_index * half_blocks, half_blocks, 0)
    leaf_all = lax.dynamic_slice_in_dim(bounds_leaf, col_id, 1, 0)[0]
    leaf_slots = leaf_all.shape[0] // row_total
    leaf_list = lax.dynamic_slice_in_dim(leaf_all, row_id * leaf_slots, leaf_slots, 0)
    wanted = jnp.concatenate([mid_list, leaf_list])
    root_values = lax.psum_scatter(
        jnp.dot(dinv_root, rhs_root, preferred_element_type=jnp.float32),
        "col",
        scatter_dimension=0,
        tiled=True,
    ).astype(jnp.bfloat16)
    picked = pick_blocks(lax.all_gather(root_values, ("row", "col"), axis=0, tiled=True), wanted)
    bound_mid = picked[:half_blocks].reshape(half_blocks * BLOCK, rhs_width).astype(jnp.bfloat16)
    root_side = picked[half_blocks:]
    mid_part = transposed_product(coup_mid, bound_mid)
    mid_terms = mid_part + partner(mid_part, "row", 0)
    rhs_here = lax.dynamic_slice_in_dim(rhs_mid, front_mid, 1, 0)[0]
    shift_mid = (rhs_here - mid_terms).astype(jnp.bfloat16)
    mid_values = lax.psum_scatter(
        jnp.dot(dinv_mid, shift_mid, preferred_element_type=jnp.float32),
        "col",
        scatter_dimension=0,
        tiled=True,
    ).astype(jnp.bfloat16)
    half_rows = lax.all_gather(mid_values, "col", axis=0, tiled=True)
    half_count = half_rows.shape[0] // BLOCK
    half_flat = half_rows.reshape(half_count, BLOCK * rhs_width)
    local_ids = leaf_all - root_total - half_index * half_count
    owns_parent = lax.dynamic_slice_in_dim(parents, col_id, 1, 0)[0] == front_mid
    choose = (
        (local_ids[:, None] == jnp.arange(half_count, dtype=jnp.int32)[None, :]) & owns_parent
    ).astype(jnp.bfloat16)
    from_parent = lax.psum_scatter(
        jnp.dot(choose, half_flat, preferred_element_type=jnp.float32).astype(jnp.bfloat16),
        "row",
        scatter_dimension=0,
        tiled=True,
    ).astype(jnp.float32)
    bound_leaf = (
        (root_side + from_parent).reshape(leaf_slots * BLOCK, rhs_width).astype(jnp.bfloat16)
    )
    coup_here = coup_leaf[0]
    leaf_sum = lax.psum_scatter(
        transposed_product(coup_here, bound_leaf), "row", scatter_dimension=0, tiled=True
    )
    shift_leaf = (rhs_leaf[0] - leaf_sum).astype(jnp.bfloat16)
    dinv_here = dinv_leaf[0]
    leaf_values = lax.psum_scatter(
        jnp.dot(dinv_here, shift_leaf, preferred_element_type=jnp.float32),
        "row",
        scatter_dimension=0,
        tiled=True,
    ).astype(jnp.bfloat16)
    return (root_values, mid_values, leaf_values[None])


def solution(mesh):
    return jax.shard_map(
        shards,
        mesh=mesh,
        in_specs=(
            P("row", "col"),
            P("col", None),
            P("row", "col"),
            P("row", "col"),
            P(None, "col", None),
            P("col", None, "row"),
            P("col", "row", None),
            P("col", "row", None),
            P(),
            P(),
            P(),
        ),
        out_specs=(P(("row", "col"), None), P(("row", "col"), None), P("col", "row", None)),
        check_vma=False,
    )
```

profile of v0, /device:TPU:1, one launch (start us, length us, event | category | flops | bytes accessed | tf_op | source)
XLA Modules:
  0.0 574.5 jit_solution(10128190450903657493)
XLA Ops:
  7.2 6.5 %fusion.20 = f32[2048,384]{1,0:T(8,128)} fusion(bf16[2048,1024]{1,0:T(8,128)(2,1)} %param.11, bf16[1024,384]{1,0:T(8,128)(2,1)} %param.12), kind=kOutput, calls=%fused_computation.30 | convolution fusion | flops 1610612736 | bytes 8126464 | tf_op jit(solution)/shard_map/dot_general | solution.py:58
  13.8 78.4 %reduce-scatter.7.cloned.1.call-done = f32[128,384]{1,0:T(8,128)} async-done(((f32[2048,384]{1,0:T(8,128)}), f32[128,384]{1,0:T(8,128)}) %reduce-scatter.7.cloned.1.call-update) | async-done | bytes 196624 | tf_op jit(solution)/shard_map/reduce_scatter | solution.py:57
  92.1 1.6 convert_element_type.45
  95.4 74.7 %all-gather.3.cloned.1.call-done = bf16[16384,384]{1,0:T(8,128)(2,1)} async-done(((bf16[128,384]{1,0:T(8,128)(2,1)}), bf16[16384,384]{1,0:T(8,128)(2,1)}) %all-gather.3.cloned.1.call-update) | async-done | bytes 12582928 | tf_op jit(solution)/shard_map/all_gather | solution.py:63
  170.1 16.4 %reshape.33 = bf16[128,49152]{1,0:T(8,128)(2,1)} reshape(bf16[16384,384]{1,0:T(8,128)(2,1)} %all-gather.3.cloned.1.call-done) | data formatting | bytes 25165824 | tf_op jit(solution)/shard_map/reshape | solution.py:18
  186.5 5.6 fusion.16
  192.1 3.0 copy-done.2
  195.2 2.1 slice.16
  197.2 4.8 convert_element_type.48
  202.0 5.0 convolution_bitcast_fusion.2
  207.6 1.8 collective-permute-done
  209.4 6.7 %convolution_bitcast_fusion.1 = f32[4096,384]{0,1:T(8,128)} fusion(bf16[4096,512]{1,0:T(8,128)(2,1)} %param.13, f32[512,384]{0,1:T(8,128)S(1)} %convolution_bitcast_fusion.2, f32[512,384]{0,1:T(8,128)S(1)} %collective-permute-done, bf16[1,512,384]{1,2,0:T(8,128)(2,1)S(1)} %copy.26), kind=kOutput, calls=%fused_computation.6 | convolution fusion | flops 1611399168 | bytes 12451840 | tf_op jit(solution)/shard_map/dot_general | solution.py:71
  216.1 79.4 %reduce-scatter.9.cloned.1.call-done = f32[256,384]{0,1:T(8,128)} async-done(((f32[4096,384]{0,1:T(8,128)}), f32[256,384]{0,1:T(8,128)}) %reduce-scatter.9.cloned.1.call-update) | async-done | bytes 393232 | tf_op jit(solution)/shard_map/reduce_scatter | solution.py:70
  295.5 1.7 convert_element_type.50
  299.2 50.5 %all-gather.5.cloned.1.call-done = bf16[4096,384]{0,1:T(8,128)(2,1)} async-done(((bf16[256,384]{0,1:T(8,128)(2,1)}), bf16[4096,384]{0,1:T(8,128)(2,1)}) %all-gather.5.cloned.1.call-update) | async-done | bytes 3145744 | tf_op jit(solution)/shard_map/all_gather | solution.py:76
  349.7 4.7 copy.23
  354.4 4.9 reshape.34
  359.3 5.4 convolution_convert_fusion
  364.8 40.3 %fusion = bf16[8,49152]{1,0:T(8,128)(2,1)S(1)} fusion(bf16[48,49152]{1,0:T(8,128)(2,1)} %convolution_convert_fusion), kind=kCustom, calls=%all-reduce-scatter | all-reduce-scatter fusion | flops 3145729 | bytes 5505536
  405.0 4.4 collective-permute-start.1
  409.6 3.2 collective-permute-start.2
  414.1 21.1 %collective-permute-done.2 = bf16[6,49152]{1,0:T(8,128)(2,1)S(1)} collective-permute-done((bf16[6,49152]{1,0:T(8,128)(2,1)S(1)}, bf16[6,49152]{1,0:T(8,128)(2,1)S(1)}, u32[]{:S(2)}, u32[]{:S(2)}) %collective-permute-start.2) | collective-permute-done | bytes 589856
  435.2 28.4 %concatenate.4 = bf16[22,49152]{1,0:T(8,128)(2,1)} concatenate(bf16[6,49152]{1,0:T(8,128)(2,1)S(1)} %collective-permute-done.2, bf16[8,49152]{1,0:T(8,128)(2,1)S(1)} %collective-permute-done.1, bf16[8,49152]{1,0:T(8,128)(2,1)S(1)} %fusion), dimensions={0} | concatenate | bytes 4325376
  463.6 2.2 fusion.7
  466.7 8.1 %fusion.3 = f32[4096,384]{0,1:T(8,128)} fusion(bf16[768,384]{1,0:T(8,128)(2,1)S(1)} %convert_element_type.56, bf16[1,768,4096]{2,1,0:T(8,128)(2,1)} %param.17), kind=kOutput, calls=%fused_computation.4 | convolution fusion | flops 2415919104 | bytes 13172736 | tf_op jit(solution)/shard_map/dot_general | solution.py:25
  474.9 0.9 copy-done.4
  476.0 40.2 %reduce-scatter.11.cloned.1.call-done = f32[512,384]{0,1:T(8,128)} async-done(((f32[4096,384]{0,1:T(8,128)}), f32[512,384]{0,1:T(8,128)}) %reduce-scatter.11.cloned.1.call-update) | async-done | bytes 786448 | tf_op jit(solution)/shard_map/reduce_scatter | solution.py:94
  516.2 6.9 %convolution_bitcast_fusion = f32[4096,384]{0,1:T(8,128)} fusion(bf16[1,4096,512]{2,1,0:T(8,128)(2,1)} %param.16, f32[512,384]{0,1:T(8,128)} %reduce-scatter.11.cloned.1.call-done, bf16[1,512,384]{1,2,0:T(8,128)(2,1)S(1)} %copy.22), kind=kOutput, calls=%fused_computation.5 | convolution fusion | flops 1611202560 | bytes 11665408 | tf_op jit(solution)/shard_map/dot_general | solution.py:100
  523.1 0.9 copy-done.3
  524.9 40.6 %reduce-scatter.13.cloned.1.call-done = f32[512,384]{0,1:T(8,128)} async-done(((f32[4096,384]{0,1:T(8,128)}), f32[512,384]{0,1:T(8,128)}) %reduce-scatter.13.cloned.1.call-update) | async-done | bytes 786448 | tf_op jit(solution)/shard_map/reduce_scatter | solution.py:99
  565.5 1.2 convert_bitcast_fusion
  566.7 0.9 copy.25
  (37 shorter events, 6.5 us)
Async XLA Ops:
  7.2 200.2 %copy-start = (bf16[4,512,384]{2,1,0:T(8,128)(2,1)S(1)}, bf16[4,512,384]{2,1,0:T(8,128)(2,1)}, u32[]{:S(2)}) copy-start(bf16[4,512,384]{2,1,0:T(8,128)(2,1)} %param.15) | copy-start | bytes 4718596
  7.2 84.9 %reduce-scatter.7.cloned.1.call-start = ((), (), s32[]{:S(2)}) async-start(), calls=%async_computation.4 | async-start | bytes 3342336 | tf_op jit(solution)/shard_map/reduce_scatter | solution.py:57
  13.7 156.4 %all-gather.3.cloned.1.call-start = ((), (), s32[]{:S(2)}) async-start(), calls=%async_computation.5 | async-start | bytes 12681216 | tf_op jit(solution)/shard_map/all_gather | solution.py:63
  93.7 201.8 %reduce-scatter.9.cloned.1.call-start = ((), (), s32[]{:S(2)}) async-start(), calls=%async_computation.6 | async-start | bytes 6684672 | tf_op jit(solution)/shard_map/reduce_scatter | solution.py:70
  192.1 3.0 copy-start.2
  207.0 2.4 collective-permute-start
  216.1 81.2 %copy-start.6 = (s32[16]{0:T(128)S(1)}, s32[16]{0:T(128)}, u32[]{:S(2)}) copy-start(s32[16]{0:T(128)} %param.21) | copy-start | bytes 196
  216.1 133.6 %all-gather.5.cloned.1.call-start = ((), (), s32[]{:S(2)}) async-start(), calls=%async_computation.7 | async-start | bytes 3342336 | tf_op jit(solution)/shard_map/all_gather | solution.py:76
  297.2 219.0 %reduce-scatter.11.cloned.1.call-start = ((), (), s32[]{:S(2)}) async-start(), calls=%async_computation.8 | async-start | bytes 7077888 | tf_op jit(solution)/shard_map/reduce_scatter | solution.py:94
  364.8 48.0 %copy-start.5 = (u32[128]{0:T(128)S(1)}, u32[128]{0:T(128)}, u32[]{:S(2)}) copy-start(u32[128]{0:T(128)} %constant.79) | copy-start | bytes 1540
  405.0 30.2 %collective-permute-start.1 = (bf16[8,49152]{1,0:T(8,128)(2,1)S(1)}, bf16[8,49152]{1,0:T(8,128)(2,1)S(1)}, u32[]{:S(2)}, u32[]{:S(2)}) collective-permute-start(bf16[8,49152]{1,0:T(8,128)(2,1)S(1)} %fusion), channel_id=1, source_target_pairs={{0,16},{16,32},{32,48},{48,64},{64,80},{80,96},{96,112},{1,17},{17... | collective-permute-start | bytes 2359304
  409.6 25.6 %collective-permute-start.2 = (bf16[6,49152]{1,0:T(8,128)(2,1)S(1)}, bf16[6,49152]{1,0:T(8,128)(2,1)S(1)}, u32[]{:S(2)}, u32[]{:S(2)}) collective-permute-start(bf16[6,49152]{1,0:T(8,128)(2,1)S(1)} %slice.11), channel_id=1, source_target_pairs={{0,32},{16,48},{32,64},{48,80},{64,96},{80,112},{1,33},{17,49},{33... | collective-permute-start | bytes 1769480
  474.8 1.0 copy-start.4
  474.8 90.7 %reduce-scatter.13.cloned.1.call-start = ((), (), s32[]{:S(2)}) async-start(), calls=%async_computation.9 | async-start | bytes 7077888 | tf_op jit(solution)/shard_map/reduce_scatter | solution.py:99
  523.1 0.9 copy-start.3
  523.1 44.5 %copy-start.1 = (bf16[4,512,384]{2,1,0:T(8,128)(2,1)S(1)}, bf16[4,512,384]{2,1,0:T(8,128)(2,1)}, u32[]{:S(2)}) copy-start(bf16[4,512,384]{2,1,0:T(8,128)(2,1)} %param.15) | copy-start | bytes 4718596
Sparse Core Ops, SparseCore 0:
  13.8 78.2 reduce-scatter.6
  95.8 74.2 all-gather.2
  216.2 79.2 reduce-scatter.8
  298.1 51.5 all-gather.4
  475.0 41.2 reduce-scatter.10
  523.3 42.1 reduce-scatter.12
where the time goes:
time: 577 us; the launch traced here: 574 us
  waiting for transfers between devices  387 us (67%)
  local copies, waits for them, and re-layouts  72.1 us (12%)
  matrix products  44.2 us (8%)
  blocking collectives  40.3 us (7%)
  between operations  15.6 us (3%)
  starting transfers between devices  8.16 us (1%)
  other arithmetic  7.39 us (1%)
    reduce_scatter x1, waiting for transfers between devices, shards(): lax.psum_scatter(jnp.dot(dinv_mid, shift_mid, preferred_element_type=jnp....  79.4 us
    reduce_scatter x1, waiting for transfers between devices, shards(): lax.psum_scatter(jnp.dot(dinv_root, rhs_root, preferred_element_type=jnp....  78.4 us
    all_gather x1, waiting for transfers between devices, shards(): lax.all_gather(root_values, ('row', 'col'), axis=0, tiled=True)  74.7 us
    all_gather x1, waiting for transfers between devices, shards(): half_rows = lax.all_gather(mid_values, 'col', axis=0, tiled=True)  50.5 us
    reduce_scatter x1, waiting for transfers between devices, shards(): lax.psum_scatter(jnp.dot(dinv_here, shift_leaf, preferred_element_type=jn...  40.6 us
    unnamed x1, blocking collectives  40.3 us
    reduce_scatter x1, waiting for transfers between devices, shards(): lax.psum_scatter(transposed_product(coup_here, bound_leaf), 'row', scatte...  40.2 us
    unnamed x21, local copies, waits for them, and re-layouts  36.2 us
  transfers between devices with their start and end apart: 9, of which 8 were waited for; matrix products, arithmetic and copies ran while one was open for 1% of the time, Pallas kernels for 0%

commit v1 on v0

v1 whole, which is shorter than its diff:
```python
import functools

import jax
import jax.numpy as jnp
from jax import lax
from jax.experimental import pallas as pl
from jax.experimental.pallas import tpu as pltpu
from jax.sharding import PartitionSpec as P

MESH = pl.DeviceIdType.MESH
BF = jnp.bfloat16
F32 = jnp.float32
BLOCK = 128
NT = (((1,), (1,)), ((), ()))


def position():
    row, col = lax.axis_index("row"), lax.axis_index("col")
    return row, col, lax.div(row, 2), lax.rem(row, 2), lax.div(col, 4), lax.rem(col, 4)


def ring(p, d):
    return lax.rem(p + d, 4)


class Links:
    def __init__(self, send, recv):
        self.send, self.recv, self.made = send, recv, []

    def __call__(self, src, dst, device):
        i = len(self.made)
        copy = pltpu.make_async_remote_copy(
            src_ref=src,
            dst_ref=dst,
            send_sem=self.send.at[i],
            recv_sem=self.recv.at[i],
            device_id=device,
            device_id_type=MESH,
        )
        copy.start()
        self.made.append(copy)
        return copy

    def drain(self):
        for copy in self.made:
            copy.wait_send()


def greet(peers):
    barrier = pltpu.get_barrier_semaphore()
    for peer in peers:
        pl.semaphore_signal(barrier, inc=1, device_id=peer, device_id_type=MESH)
    pl.semaphore_wait(barrier, len(peers))


def ring_sum(links, value, up, down, s, rf, rn, p):
    s[1, 0] = value(2, 0).astype(BF)
    far_up = links(s.at[1, 0], rf.at[0], up)
    s[1, 1] = value(2, 1).astype(BF)
    far_down = links(s.at[1, 1], rf.at[1], down)
    s[0, 1] = value(1, 1).astype(BF)
    last = [links(s.at[0, 1], rn.at[0, 1], up)]
    s[2, 0] = value(3, 0).astype(BF)
    last.append(links(s.at[2, 0], rn.at[1, 0], down))
    p[0] = value(1, 0)
    p[1] = value(3, 1)
    far_up.wait_recv()
    s[0, 0] = (p[0] + rf[0].astype(F32)).astype(BF)
    last.append(links(s.at[0, 0], rn.at[0, 0], up))
    far_down.wait_recv()
    s[2, 1] = (p[1] + rf[1].astype(F32)).astype(BF)
    last.append(links(s.at[2, 1], rn.at[1, 1], down))
    p[2] = value(0, 0)
    p[3] = value(0, 1)
    for copy in last:
        copy.wait_recv()
    return [p[2 + h] + rn[0, h].astype(F32) + rn[1, h].astype(F32) for h in range(2)]


def root_kernel(
    bm, bl, root_t, mid_t, w_hbm, c_hbm,
    out_root, out_shift, out_side,
    w, c, ra, s1, rf1, rn1, p1, y1, s2, rf2, rn2, p2, bt, ex, exr,
    local, send, recv,
):
    row, col, x, k, z, y = position()
    a, b = k * z + (1 - k) * y, k * y + (1 - k) * z

    def chip(a_, b_):
        return k * (4 * a_ + b_) + (1 - k) * (4 * b_ + a_)

    load_w = pltpu.make_async_copy(w_hbm, w, local.at[0])
    load_c = pltpu.make_async_copy(c_hbm, c, local.at[1])
    load_w.start()
    load_c.start()
    along = {
        "x": lambda d: (2 * ring(x, d) + k, col),
        "y": lambda d: (row, 4 * z + ring(y, d)),
        "z": lambda d: (row, 4 * ring(z, d) + y),
    }
    partner = (2 * x + 1 - k, col)
    greet([along[axis](d) for axis in "xyz" for d in (1, 3)] + [partner])
    links = Links(send, recv)
    load_w.wait()

    def root_term(d, h):
        ids = [chip(ring(a, d), 2 * h + j) for j in range(2)]
        rows = jnp.concatenate(
            [w[pl.ds(pl.multiple_of(i * BLOCK, BLOCK), BLOCK), :] for i in ids], axis=0
        )
        return lax.dot_general(root_t[...], rows, NT, preferred_element_type=F32)

    halves = ring_sum(
        links, root_term, (row, chip(ring(a, 1), b)), (row, chip(ring(a, 3), b)), s1, rf1, rn1, p1
    )
    for h in range(2):
        for j in range(2):
            y1[2 * h + j] = halves[h][:, j * BLOCK : (j + 1) * BLOCK]
    tall = y1.shape[1] // 2
    halves = ring_sum(
        links,
        lambda d, h: y1[ring(b, d), h * tall : (h + 1) * tall, :],
        (row, chip(a, ring(b, 1))),
        (row, chip(a, ring(b, 3))),
        s2, rf2, rn2, p2,
    )
    for h in range(2):
        half = halves[h].astype(BF)
        ra[x, k, z, y, h * tall : (h + 1) * tall, :] = half
        out_root[h * tall : (h + 1) * tall, :] = half

    third = ra.shape[4] // 3
    here = {"x": x, "y": y, "z": z}

    def view(part, done, axis, at, half):
        index = []
        lead = True
        split = half is not None
        for name in ("x", "k", "z", "y"):
            if name == "k":
                index.append(k)
            elif name == axis:
                index.append(at)
            elif name in done:
                if split and lead:
                    index.append(pl.ds(2 * half, 2))
                else:
                    index.append(slice(None))
                lead = False
            else:
                index.append(here[name])
        if split and not done:
            index.append(pl.ds(part * third + half * (third // 2), third // 2))
        else:
            index.append(pl.ds(part * third, third))
        return ra.at[tuple(index)]

    orders = ("xyz", "yzx", "zxy")
    shared = []

    def share(ref):
        shared.append(links(ref, ref, partner))

    for phase in range(3):
        state = []
        for part, order in enumerate(orders):
            axis, done, at = order[phase], order[:phase], here[order[phase]]
            own = view(part, done, axis, at, None)
            state.append((links(own, own, along[axis](1)), links(own, own, along[axis](3))))
            if phase == 2:
                share(own)
        onward = []
        for part, order in enumerate(orders):
            axis, done, at = order[phase], order[:phase], here[order[phase]]
            state[part][0].wait_recv()
            got = view(part, done, axis, ring(at, 3), 0)
            first = links(got, got, along[axis](1))
            state[part][1].wait_recv()
            got = view(part, done, axis, ring(at, 1), 1)
            onward.append((first, links(got, got, along[axis](3))))
            if phase == 2:
                share(view(part, done, axis, ring(at, 3), None))
                share(view(part, done, axis, ring(at, 1), None))
        for part, order in enumerate(orders):
            axis, done, at = order[phase], order[:phase], here[order[phase]]
            for half in range(2):
                onward[part][half].wait_recv()
                if phase == 2:
                    share(view(part, done, axis, ring(at, 2), half))
    for copy in shared:
        copy.wait_recv()

    def root_block(v):
        return ra[lax.div(v, 32), lax.rem(lax.div(v, 16), 2), lax.rem(lax.div(v, 4), 4), lax.rem(v, 4)]

    load_c.wait()
    count = bm.shape[1] // 2
    group = bt.shape[1] // BLOCK
    for g in range(count // group):
        for j in range(group):
            bt[:, j * BLOCK : (j + 1) * BLOCK] = root_block(bm[x, k * count + g * group + j])
        rows = group * BLOCK
        term = jnp.dot(bt[...], c[g * rows : (g + 1) * rows, :], preferred_element_type=F32)
        if g == 0:
            ex[...] = term
        else:
            ex[...] += term
    swap = links(ex, exr, partner)
    slots = out_side.shape[0]
    for i in range(slots):
        out_side[i] = root_block(jnp.minimum(bl[col, row * slots + i], 127))
    swap.wait_recv()
    out_shift[...] = (mid_t[...].astype(F32) - (ex[...] + exr[...])).astype(BF)
    links.drain()


def mid_kernel(
    bl, parents, shift, side, w_hbm,
    out_mid, out_bound,
    w, s1, rf1, rn1, p1, y1, s2, rf2, rn2, p2, m4, r, ts, t, u, bb,
    local, send, recv,
):
    row, col, x, k, z, y = position()
    a, b = k * z + (1 - k) * y, k * y + (1 - k) * z

    def chip(a_, b_):
        return k * (4 * a_ + b_) + (1 - k) * (4 * b_ + a_)

    load_w = pltpu.make_async_copy(w_hbm, w, local.at[0])
    load_w.start()
    offsets = [(i, j) for i in (2, 1, 3, 0) for j in (2, 1, 3, 0) if (i, j) != (0, 0)]

    def plane(dz, dy):
        return 4 * ring(z, dz) + ring(y, dy)

    partner = (2 * x + 1 - k, col)
    greet(
        [(row, plane(*o)) for o in offsets]
        + [(2 * ring(x, d) + k, col) for d in (1, 2, 3)]
        + [partner]
    )
    links = Links(send, recv)
    load_w.wait()
    wide = 2 * BLOCK

    def mid_term(d, h):
        ids = [chip(ring(a, d), 2 * h + j) for j in range(2)]
        rows = jnp.concatenate(
            [w[pl.ds(pl.multiple_of(i * wide, wide), wide), :] for i in ids], axis=0
        )
        return lax.dot_general(shift[...], rows, NT, preferred_element_type=F32)

    halves = ring_sum(
        links, mid_term, (row, chip(ring(a, 1), b)), (row, chip(ring(a, 3), b)), s1, rf1, rn1, p1
    )
    for h in range(2):
        for j in range(2):
            y1[2 * h + j] = halves[h][:, j * wide : (j + 1) * wide]
    tall = y1.shape[1] // 2
    halves = ring_sum(
        links,
        lambda d, h: y1[ring(b, d), h * tall : (h + 1) * tall, :],
        (row, chip(a, ring(b, 1))),
        (row, chip(a, ring(b, 3))),
        s2, rf2, rn2, p2,
    )
    quarter = tall // 2
    for h in range(2):
        half = halves[h].astype(BF)
        out_mid[h * tall : (h + 1) * tall, :] = half
        for i in range(2):
            for j in range(2):
                m4[2 * h + i, j] = half[
                    i * quarter : (i + 1) * quarter, j * BLOCK : (j + 1) * BLOCK
                ]
    moved = []
    for d in (2, 1, 3):
        q = ring(x, d)
        moved.append(links(m4.at[q], r.at[x], (2 * q + k, col)))
    r[x] = m4[x]
    for copy in moved:
        copy.wait_recv()
    moved = []
    for i, (dz, dy) in enumerate(offsets):
        to = plane(dz, dy)
        ts[i] = r[parents[to]]
        moved.append(links(ts.at[i], t.at[k, col], (row, to)))
    t[k, col] = r[parents[col]]
    shared = [links(t.at[k, col], t.at[k, col], partner)]
    for copy, (dz, dy) in zip(moved, offsets):
        copy.wait_recv()
        got = t.at[k, plane(4 - dz, 4 - dy)]
        shared.append(links(got, got, partner))
    for copy in shared:
        copy.wait_recv()
    slots = side.shape[0]

    def parent_block(v):
        m = jnp.maximum(v - 128, 0)
        return t[lax.div(m, 32), lax.div(lax.rem(m, 32), 2), lax.rem(m, 2)]

    moved = []
    for d in (2, 1, 3):
        q = ring(x, d)
        for i in range(slots):
            u[d - 1, i] = parent_block(bl[col, (2 * q + k) * slots + i])
        moved.append(links(u.at[d - 1], bb.at[x], (2 * q + k, col)))
    for i in range(slots):
        bb[x, i] = parent_block(bl[col, row * slots + i])
    for copy in moved:
        copy.wait_recv()
    for i in range(slots):
        from_root = bl[col, row * slots + i] < 128
        for q in range(4):
            span = slice(q * quarter, (q + 1) * quarter)
            out_bound[span, i * BLOCK : (i + 1) * BLOCK] = jnp.where(
                from_root, side[i, span, :].astype(F32), bb[q, i].astype(F32)
            ).astype(BF)
    links.drain()


def leaf_kernel(
    bound, leaf_t, c_hbm, w_hbm,
    out_leaf,
    c, w, own, sp, rp1, rp2, s1, rf1, rn1, s2, rf2, rn2, p, shift,
    local, send, recv,
):
    row, col, x, k, z, y = position()
    load_c = pltpu.make_async_copy(c_hbm, c, local.at[0])
    load_w = pltpu.make_async_copy(w_hbm, w, local.at[1])
    load_c.start()
    load_w.start()
    partner = (2 * x + 1 - k, col)
    up, down = (2 * ring(x, 1) + k, col), (2 * ring(x, 3) + k, col)
    greet([partner, up, down])
    links = Links(send, recv)
    size = own.shape[2]
    tall = own.shape[1] // 2

    def chunk(q, core):
        return pl.ds(pl.multiple_of((2 * q + core) * size, size), size)

    def scatter(product, rp, stage, s, rf, rn):
        order = [2, 1, 3, 0]
        sent, ready = {}, set()

        def make(d):
            q = ring(x, d)
            sp[stage, d] = product(chunk(q, 1 - k)).astype(BF)
            sent[d] = links(sp.at[stage, d], rp.at[d], partner)
            own[d] = product(chunk(q, k))

        def value(d, h):
            upto = min(order.index(d) + 1, 3)
            for e in order[: upto + 1]:
                if e not in sent:
                    make(e)
            if d not in ready:
                sent[d].wait_recv()
                ready.add(d)
            rows = slice(h * tall, (h + 1) * tall)
            return own[d, rows, :] + rp[d, rows, :].astype(F32)

        return ring_sum(links, value, up, down, s, rf, rn, p)

    load_c.wait()
    halves = scatter(
        lambda span: jnp.dot(bound[...], c[:, span], preferred_element_type=F32),
        rp1, 0, s1, rf1, rn1,
    )
    for h in range(2):
        rows = slice(h * tall, (h + 1) * tall)
        shift[rows, :] = (leaf_t[rows, :].astype(F32) - halves[h]).astype(BF)
    load_w.wait()
    halves = scatter(
        lambda span: lax.dot_general(shift[...], w[span, :], NT, preferred_element_type=F32),
        rp2, 1, s2, rf2, rn2,
    )
    for h in range(2):
        out_leaf[h * tall : (h + 1) * tall, :] = halves[h].astype(BF)
    links.drain()


VM = pl.BlockSpec(memory_space=pltpu.VMEM)
SM = pl.BlockSpec(memory_space=pltpu.SMEM)
ANY = pl.BlockSpec(memory_space=pl.ANY)


def call(kernel, number, in_specs, outs, scratch, copies, args):
    return pl.pallas_call(
        kernel,
        out_shape=tuple(jax.ShapeDtypeStruct(shape, BF) for shape in outs),
        in_specs=in_specs,
        out_specs=(VM,) * len(outs),
        scratch_shapes=[pltpu.VMEM(shape, kind) for shape, kind in scratch]
        + [
            pltpu.SemaphoreType.DMA((2,)),
            pltpu.SemaphoreType.DMA((copies,)),
            pltpu.SemaphoreType.DMA((copies,)),
        ],
        compiler_params=pltpu.CompilerParams(
            collective_id=number, has_side_effects=True, vmem_limit_bytes=58 * 1024 * 1024
        ),
    )(*args)


def ring_scratch(half):
    return [((3, 2) + half, BF), ((2,) + half, BF), ((2, 2) + half, BF), ((4,) + half, F32)]


def shards(
    dinv_root, rhs_root, dinv_mid, coup_mid, rhs_mid, dinv_leaf, coup_leaf, rhs_leaf,
    bounds_mid, bounds_leaf, parents,
):
    front = lax.div(lax.axis_index("row"), 2)
    n = rhs_root.shape[1]
    slots = bounds_leaf.shape[1] // 8
    sep_mid, sep_leaf = rhs_mid.shape[1], rhs_leaf.shape[1]
    root_t = rhs_root.T
    mid_t = lax.dynamic_index_in_dim(rhs_mid, front, 0, keepdims=False).T
    leaf_t = rhs_leaf[0].T
    wide = 2 * BLOCK
    root_out, shift, side = call(
        root_kernel, 0,
        [SM, SM, VM, VM, ANY, ANY],
        [(n, BLOCK), (n, sep_mid), (slots, n, BLOCK)],
        [(dinv_root.shape, BF), (coup_mid.shape, BF), ((4, 2, 4, 4, n, BLOCK), BF)]
        + ring_scratch((n, wide))
        + [((4, n, BLOCK), F32)]
        + ring_scratch((n // 2, BLOCK))
        + [((n, 8 * BLOCK), BF), ((n, sep_mid), F32), ((n, sep_mid), F32)],
        64,
        (bounds_mid, bounds_leaf, root_t, mid_t, dinv_root, coup_mid),
    )
    quarter = n // 4
    mid_out, bound = call(
        mid_kernel, 1,
        [SM, SM, VM, VM, ANY],
        [(n, wide), (n, slots * BLOCK)],
        [(dinv_mid.shape, BF)]
        + ring_scratch((n, 2 * wide))
        + [((4, n, wide), F32)]
        + ring_scratch((n // 2, wide))
        + [
            ((4, 2, quarter, BLOCK), BF),
            ((4, 2, quarter, BLOCK), BF),
            ((15, 2, quarter, BLOCK), BF),
            ((2, 16, 2, quarter, BLOCK), BF),
            ((3, slots, quarter, BLOCK), BF),
            ((4, slots, quarter, BLOCK), BF),
        ],
        64,
        (bounds_leaf, parents, shift, side, dinv_mid),
    )
    (leaf_out,) = call(
        leaf_kernel, 2,
        [VM, VM, ANY, ANY],
        [(n, sep_leaf)],
        [
            (coup_leaf.shape[1:], BF),
            (dinv_leaf.shape[1:], BF),
            ((4, n, sep_leaf), F32),
            ((2, 4, n, sep_leaf), BF),
            ((4, n, sep_leaf), BF),
            ((4, n, sep_leaf), BF),
        ]
        + ring_scratch((n // 2, sep_leaf))[:3]
        + ring_scratch((n // 2, sep_leaf))
        + [((n, sep_leaf), BF)],
        32,
        (bound, leaf_t, coup_leaf[0], dinv_leaf[0]),
    )
    return root_out.T, mid_out.T, leaf_out.T[None]


def solution(mesh):
    return jax.shard_map(
        shards,
        mesh=mesh,
        in_specs=(
            P("row", "col"),
            P("col", None),
            P("row", "col"),
            P("row", "col"),
            P(None, "col", None),
            P("col", None, "row"),
            P("col", "row", None),
            P("col", "row", None),
            P(),
            P(),
            P(),
        ),
        out_specs=(P(("row", "col"), None), P(("row", "col"), None), P("col", "row", None)),
        check_vma=False,
    )
```

time: 577 us -> 174 us (0.30)
  waiting for transfers between devices: 387 us -> 0 us
  Pallas kernels: 0 us -> 164 us
  local copies, waits for them, and re-layouts: 72.1 us -> 9.14 us
  matrix products: 44.2 us -> 0 us
  blocking collectives: 40.3 us -> 0 us
  between operations: 15.6 us -> 0.7 us
  starting transfers between devices: 8.16 us -> 0 us
  other arithmetic: 7.39 us -> 0 us
    reduce_scatter x4 -> x0, waiting for transfers between devices: 239 us -> none  [the longest x1 79.4 us: shards(): lax.psum_scatter(jnp.dot(dinv_mid, shift_mid, preferred_element_type=jnp....]
    pallas_call x0 -> x3, Pallas kernels: none -> 164 us  [call(): pl.pallas_call(kernel, out_shape=tuple((jax.ShapeDtypeStruct(shape, BF) f...]
    all_gather x2 -> x0, waiting for transfers between devices: 125 us -> none  [the longest x1 74.7 us: shards(): lax.all_gather(root_values, ('row', 'col'), axis=0, tiled=True)]
    dot_general x7 -> x0, matrix products: 44.2 us -> none  [the longest x2 13 us: transposed_product(): lax.dot_general(coupling, boundary, (((0,), (0,)), ((), ())), preferred_e...]
    unnamed x1 -> x0, blocking collectives: 40.3 us -> none
    unnamed x21 -> x13, local copies, waits for them, and re-layouts: 36.2 us -> 8.16 us
    reshape x2 -> x0, local copies, waits for them, and re-layouts: 21.3 us -> none  [the longest x1 16.4 us: pick_blocks(): flat_blocks = shard_rows.reshape(block_count, BLOCK * shard_rows.shape[1])]
    unnamed x8 -> x0, waiting for transfers between devices: 21.2 us -> none
  transfers between devices with their start and end apart: 9 -> 0, of which waited for: 8 -> 0; matrix products, arithmetic and copies ran while one was open for 1% -> 0% of each run, Pallas kernels for 0% -> 0%
where the time goes in v1:
time: 174 us
  Pallas kernels  164 us (94%)
  local copies, waits for them, and re-layouts  9.14 us (5%)
    pallas_call x3, Pallas kernels, call(): pl.pallas_call(kernel, out_shape=tuple((jax.ShapeDtypeStruct(shape, BF) f...  164 us
    unnamed x13, local copies, waits for them, and re-layouts  8.16 us

profile of v1, /device:TPU:1, one launch (start us, length us, event | category | flops | bytes accessed | tf_op | source)
XLA Modules:
  0.0 173.9 jit_solution(1298620715138703312)
XLA Ops:
  0.6 0.0 copy-start
  0.7 1.4 copy-done
  2.1 0.9 copy.15
  3.0 2.3 %copy.14 = bf16[1024,384]{0,1:T(8,128)(2,1)} copy(bf16[1024,384]{1,0:T(8,128)(2,1)} %param.12) | data formatting | bytes 1572864 | tf_op args[1]
  5.4 70.3 %shard_map.130 = (bf16[384,128]{1,0:T(8,128)(2,1)}, bf16[384,512]{1,0:T(8,128)(2,1)}, bf16[6,384,128]{2,1,0:T(8,128)(2,1)}) custom-call(s32[4,64]{1,0:T(4,128)} %bm.1, s32[16,48]{1,0:T(8,128)} %bl.3, bf16[384,1024]{1,0:T(8,128)(2,1)} %bitcast.16, bf16[384,512]{1,0:T(8,128)(2,1)} %bitcast.17, bf16[2048,1024]{1,0:T(8,128)(2,1)} %w_hbm.2, bf16[4096,512]{1,0:T(8,128)(2,1)} %c_hbm.1), custom_call_target="tpu_custom_call" | custom-call | tf_op jit(solution)/shard_map/pallas_call | solution.py:390
  75.6 0.0 copy-start.1
  75.6 53.3 %shard_map.131 = (bf16[384,256]{1,0:T(8,128)(2,1)}, bf16[384,768]{1,0:T(8,128)(2,1)}) custom-call(s32[16,48]{1,0:T(8,128)} %bl.3, s32[16]{0:T(128)} %parents.1, bf16[384,512]{1,0:T(8,128)(2,1)} %get-tuple-element.9.shift, bf16[6,384,128]{2,1,0:T(8,128)(2,1)} %get-tuple-element.10.side, bf16[4096,512]{1,0:T(8,128)(2,1)} %w_hbm.3), custom_call_target="tpu_custom_call" | custom-call | tf_op jit(solution)/shard_map/pallas_call | solution.py:390
  129.0 0.0 copy-done.1
  129.0 0.9 copy.16
  129.9 0.0 copy-start.2
  129.9 0.0 copy-start.3
  130.0 40.5 %shard_map.132 = bf16[384,512]{1,0:T(8,128)(2,1)} custom-call(bf16[384,768]{1,0:T(8,128)(2,1)} %get-tuple-element.12.bound, bf16[384,512]{1,0:T(8,128)(2,1)} %bitcast.19, bf16[768,4096]{1,0:T(8,128)(2,1)} %bitcast.14, bf16[4096,512]{1,0:T(8,128)(2,1)} %bitcast.15), custom_call_target="tpu_custom_call" | custom-call | tf_op jit(solution)/shard_map/pallas_call | solution.py:390
  170.4 1.9 %copy.19 = bf16[1,512,384]{2,1,0:T(8,128)(2,1)} copy(bf16[1,512,384]{1,2,0:T(8,128)(2,1)} %bitcast.18) | data formatting | bytes 786432
  172.3 0.0 copy-done.2
  172.3 0.8 copy.18
  173.1 0.0 copy-done.3
  173.1 0.8 copy.17
  (1 shorter events, 0.0 us)
Async XLA Ops:
  0.6 1.4 copy-start
  75.6 53.4 %copy-start.1 = (bf16[1,512,384]{2,1,0:T(8,128)(2,1)S(1)}, bf16[1,512,384]{2,1,0:T(8,128)(2,1)}, u32[]{:S(2)}) copy-start(bf16[1,512,384]{2,1,0:T(8,128)(2,1)} %param.18) | copy-start | bytes 1179652
  129.9 42.4 %copy-start.2 = (bf16[384,256]{1,0:T(8,128)(2,1)S(1)}, bf16[384,256]{1,0:T(8,128)(2,1)}, u32[]{:S(2)}) copy-start(bf16[384,256]{1,0:T(8,128)(2,1)} %get-tuple-element.11) | copy-start | bytes 589828
  129.9 43.2 %copy-start.3 = (bf16[384,128]{1,0:T(8,128)(2,1)S(1)}, bf16[384,128]{1,0:T(8,128)(2,1)}, u32[]{:S(2)}) copy-start(bf16[384,128]{1,0:T(8,128)(2,1)} %get-tuple-element.8) | copy-start | bytes 294916

commit v2 on v0

v2 whole, which is shorter than its diff:
```python
import functools

import jax
import jax.numpy as jnp
from jax import lax
from jax.experimental import pallas as pl
from jax.experimental.pallas import tpu as pltpu
from jax.sharding import PartitionSpec as P

MESH = pl.DeviceIdType.MESH
BF = jnp.bfloat16
F32 = jnp.float32
BLOCK = 128
NT = (((1,), (1,)), ((), ()))


def position():
    row, col = lax.axis_index("row"), lax.axis_index("col")
    return row, col, lax.div(row, 2), lax.rem(row, 2), lax.div(col, 4), lax.rem(col, 4)


def ring(p, d):
    return lax.rem(p + d, 4)


class Links:
    def __init__(self, send, recv):
        self.send, self.recv, self.made, self.done = send, recv, [], set()

    def __call__(self, src, dst, device):
        i = len(self.made)
        copy = pltpu.make_async_remote_copy(
            src_ref=src,
            dst_ref=dst,
            send_sem=self.send.at[i],
            recv_sem=self.recv.at[i],
            device_id=device,
            device_id_type=MESH,
        )
        copy.start()
        self.made.append(copy)
        return copy

    def sent(self, copies):
        for copy in copies:
            if id(copy) not in self.done:
                self.done.add(id(copy))
                copy.wait_send()

    def drain(self):
        self.sent(self.made)


def greet(peers):
    barrier = pltpu.get_barrier_semaphore()
    for peer in peers:
        pl.semaphore_signal(barrier, inc=1, device_id=peer, device_id_type=MESH)
    pl.semaphore_wait(barrier, len(peers))


def ring_sum(links, value, prepare, up, down, s, rf, rn, p):
    yield from prepare(2)
    s(1, 0)[...] = value(2, 0).astype(BF)
    far_up = links(s(1, 0), rf.at[0], up)
    s(1, 1)[...] = value(2, 1).astype(BF)
    far_down = links(s(1, 1), rf.at[1], down)
    yield from prepare(1)
    s(0, 1)[...] = value(1, 1).astype(BF)
    last = [links(s(0, 1), rn.at[0, 1], up)]
    yield from prepare(3)
    s(2, 0)[...] = value(3, 0).astype(BF)
    last.append(links(s(2, 0), rn.at[1, 0], down))
    if p is not None:
        for i, term in enumerate(((1, 0), (3, 1), (0, 0), (0, 1))):
            p(i)[...] = value(*term)
    kept = (lambda i, d, h: p(i)[...]) if p is not None else (lambda i, d, h: value(d, h))
    yield
    far_up.wait_recv()
    s(0, 0)[...] = (kept(0, 1, 0) + rf[0].astype(F32)).astype(BF)
    last.append(links(s(0, 0), rn.at[0, 0], up))
    yield
    far_down.wait_recv()
    s(2, 1)[...] = (kept(1, 3, 1) + rf[1].astype(F32)).astype(BF)
    last.append(links(s(2, 1), rn.at[1, 1], down))
    yield from prepare(0)
    yield
    for copy in last:
        copy.wait_recv()
    halves = [
        kept(2 + h, 0, h) + rn[0, h].astype(F32) + rn[1, h].astype(F32) for h in range(2)
    ]
    return halves, last + [far_up, far_down]


def ring_direct(links, value, to, s, rn):
    moved = []
    for d in (2, 1, 3):
        s(d - 1)[...] = value(d).astype(BF)
        moved.append(links(s(d - 1), rn.at[d - 1], to(d)))
    yield
    total = value(0)
    for copy, d in zip(moved, (2, 1, 3)):
        copy.wait_recv()
        total += rn[d - 1].astype(F32)
    return total, moved


def nothing(d):
    return
    yield


def together(programs, lag):
    turn, live = 0, list(enumerate(programs))
    while live:
        for item in list(live):
            if turn >= item[0] * lag:
                try:
                    next(item[1])
                except StopIteration:
                    live.remove(item)
        turn += 1


def kernel(
    groups, lag,
    bm, bl, parents, root_hbm, mid_hbm, leaf_hbm, w_hbm, c_hbm, dm_hbm, cl_hbm, dl_hbm,
    out_root, out_mid, out_leaf,
    root_v, root_t, mid_v, mid_t, leaf_v, leaf_t,
    w, c, dm, cl, ra_0, ra_1, pool, y1, sa, sb,
    rf1r, rn1r, rn2r, rf1m, rn1m, rn2m, exr, shift,
    m4, rq_0, rq_1, ts, t_0, t_1, u, bb, bound, sp, rp1, rp2, rf1l, rn1l, rf2l, rn2l,
    local, send, recv,
):
    row, col, x, k, z, y = position()
    a, b = k * z + (1 - k) * y, k * y + (1 - k) * z
    size = root_t.shape[0] // groups
    wide = 2 * BLOCK

    def chip(a_, b_):
        return k * (4 * a_ + b_) + (1 - k) * (4 * b_ + a_)

    def plane(dz, dy):
        return 4 * ring(z, dz) + ring(y, dy)

    def fetch(source, target, i):
        copy = pltpu.make_async_copy(source, target, local.at[i])
        copy.start()
        return copy

    loads = {"root": [fetch(root_hbm, root_v, 0)]}
    for d in (2, 1, 3, 0):
        for h in range(2):
            loads["w", d, h] = []
            for j in range(2):
                span = pl.ds(pl.multiple_of(chip(ring(a, d), 2 * h + j) * BLOCK, BLOCK), BLOCK)
                loads["w", d, h].append(fetch(w_hbm.at[span], w.at[span], 8 + 4 * d + 2 * h + j))
    offsets = [(i, j) for i in (2, 1, 3, 0) for j in (2, 1, 3, 0) if (i, j) != (0, 0)]
    partner = (2 * x + 1 - k, col)
    along = {
        "x": lambda d: (2 * ring(x, d) + k, col),
        "y": lambda d: (row, 4 * z + ring(y, d)),
        "z": lambda d: (row, 4 * ring(z, d) + y),
    }
    here = {"x": x, "y": y, "z": z}
    first_ring = (row, chip(ring(a, 1), b)), (row, chip(ring(a, 3), b))
    second_ring = lambda d: (row, chip(a, ring(b, d)))
    greet(
        [(row, plane(*o)) for o in offsets] + [along["x"](d) for d in (1, 2, 3)] + [partner]
    )
    links = Links(send, recv)
    def loaded(name):
        for copy in loads.pop(name, ()):
            copy.wait()

    loaded("root")
    root_t[...] = root_v[...].T
    passed = []

    def root_done():
        passed.append(1)
        if len(passed) == 1:
            loads["mid"] = [fetch(mid_hbm.at[x], mid_v, 1)]
            loads["c"] = [fetch(c_hbm, c, 2)]
            loads["dm"] = [fetch(dm_hbm, dm, 3)]
            loads["leaf"] = [fetch(leaf_hbm, leaf_v, 4)]
            loads["cl"] = [fetch(cl_hbm, cl, 5)]
        if len(passed) == groups:
            tall = w.shape[0]
            span = dl_hbm.shape[1]
            loads["dl"] = [
                fetch(
                    dl_hbm.at[i * tall : (i + 1) * tall], w.at[:, i * span : (i + 1) * span], 6 + i
                )
                for i in range(2)
            ]

    gathered, quarters, delivered = (ra_0, ra_1), (rq_0, rq_1), (t_0, t_1)

    def view(ra, base, part, third, done, axis, at, half):
        index = []
        lead = True
        split = half is not None
        for name in ("x", "k", "z", "y"):
            if name == "k":
                index.append(k)
            elif name == axis:
                index.append(at)
            elif name in done:
                if split and lead:
                    index.append(pl.ds(2 * half, 2))
                else:
                    index.append(slice(None))
                lead = False
            else:
                index.append(here[name])
        if split and not done:
            index.append(pl.ds(base + half * (third // 2), third // 2))
        else:
            index.append(pl.ds(base, third))
        return ra.at[tuple(index)]

    def program(g):
        lo = g * size
        ra, rq, t = gathered[g], quarters[g], delivered[g]
        rows = slice(lo, lo + size)
        tall = size // 2
        quarter = size // 4

        def root_term(d, h):
            loaded(("w", d, h))
            ids = [chip(ring(a, d), 2 * h + j) for j in range(2)]
            part = jnp.concatenate(
                [w[pl.ds(pl.multiple_of(i * BLOCK, BLOCK), BLOCK), :] for i in ids], axis=0
            )
            return lax.dot_general(root_t[rows, :], part, NT, preferred_element_type=F32)

        halves, used = yield from ring_sum(
            links, root_term, nothing, *first_ring,
            lambda i, h: sa.at[g, i, h, :, :wide], rf1r.at[g], rn1r.at[g],
            lambda i: pool.at[g, i, :, :wide],
        )
        root_done()
        for h in range(2):
            for j in range(2):
                y1[g, 2 * h + j, :, :BLOCK] = halves[h][:, j * BLOCK : (j + 1) * BLOCK]
        block, also = yield from ring_direct(
            links, lambda d: y1[g, ring(b, d), :, :BLOCK], second_ring,
            lambda i: sb.at[g, i, :, :BLOCK], rn2r.at[g],
        )
        used += also
        block = block.astype(BF)
        ra[x, k, z, y] = block
        out_root[rows, :] = block

        orders, third = ("xyz", "yzx", "zxy"), size // 3
        shared = []

        def share(ref):
            shared.append(links(ref, ref, partner))

        moved = []
        for part, order in enumerate(orders):
            own = ra.at[x, k, z, y, pl.ds(part * third, third)]
            moved += [links(own, own, along[order[0]](d)) for d in (2, 1, 3)]
        yield
        if "mid" in loads:
            loaded("mid")
            mid_t[...] = mid_v[...].T
            loaded("leaf")
            leaf_t[...] = leaf_v[...].T
        for copy in moved:
            copy.wait_recv()
        for phase in (1, 2):

            def piece(part, shift_by, half=None):
                order = orders[part]
                axis = order[phase]
                return view(
                    ra, part * third, part, third, order[:phase], axis, ring(here[axis], shift_by), half
                )

            state = []
            for part, order in enumerate(orders):
                own = piece(part, 0)
                axis = order[phase]
                state.append((links(own, own, along[axis](1)), links(own, own, along[axis](3))))
                if phase == 2:
                    share(own)
            yield
            onward = []
            for part, order in enumerate(orders):
                axis = order[phase]
                state[part][0].wait_recv()
                got = piece(part, 3, 0)
                first = links(got, got, along[axis](1))
                state[part][1].wait_recv()
                got = piece(part, 1, 1)
                onward.append((first, links(got, got, along[axis](3))))
                if phase == 2:
                    share(piece(part, 3))
                    share(piece(part, 1))
            yield
            for part in range(len(orders)):
                for half in range(2):
                    onward[part][half].wait_recv()
                    if phase == 2:
                        share(piece(part, 2, half))
        yield
        for copy in shared:
            copy.wait_recv()

        def root_block(v):
            return ra[
                lax.div(v, 32), lax.rem(lax.div(v, 16), 2), lax.rem(lax.div(v, 4), 4), lax.rem(v, 4)
            ]

        loaded("c")
        count = bm.shape[1] // 2
        for q in range(count // 16):
            for i in range(4):
                for j in range(4):
                    sp[g, i, :, j * BLOCK : (j + 1) * BLOCK] = root_block(
                        bm[x, k * count + q * 16 + i * 4 + j]
                    )
            left = jnp.concatenate([sp[g, i] for i in range(4)], axis=1)
            term = jnp.dot(
                left, c[q * 16 * BLOCK : (q + 1) * 16 * BLOCK, :], preferred_element_type=F32
            )
            if q == 0:
                pool[g, 0] = term
            else:
                pool[g, 0] += term
        swap = links(pool.at[g, 0], exr.at[g], partner)
        yield
        swap.wait_recv()
        shift[g] = (mid_t[rows, :].astype(F32) - (pool[g, 0] + exr[g])).astype(BF)
        links.sent(used + [swap])
        loaded("dm")

        def mid_term(d, h):
            ids = [chip(ring(a, d), 2 * h + j) for j in range(2)]
            part = jnp.concatenate(
                [dm[pl.ds(pl.multiple_of(i * wide, wide), wide), :] for i in ids], axis=0
            )
            return lax.dot_general(shift[g], part, NT, preferred_element_type=F32)

        halves, used = yield from ring_sum(
            links, mid_term, nothing, *first_ring,
            lambda i, h: sa.at[g, i, h], rf1m.at[g], rn1m.at[g], lambda i: pool.at[g, i],
        )
        for h in range(2):
            for j in range(2):
                y1[g, 2 * h + j] = halves[h][:, j * wide : (j + 1) * wide]
        block, also = yield from ring_direct(
            links, lambda d: y1[g, ring(b, d)], second_ring, lambda i: sb.at[g, i], rn2m.at[g]
        )
        used += also
        block = block.astype(BF)
        out_mid[rows, :] = block
        for i in range(4):
            for j in range(2):
                m4[g, i, j] = block[i * quarter : (i + 1) * quarter, j * BLOCK : (j + 1) * BLOCK]

        moved = []
        for d in (2, 1, 3):
            q = ring(x, d)
            moved.append(links(m4.at[g, q], rq.at[x], (2 * q + k, col)))
        rq[x] = m4[g, x]
        yield
        for copy in moved:
            copy.wait_recv()
        moved = []
        for i, (dz, dy) in enumerate(offsets):
            to = plane(dz, dy)
            ts[g, i] = rq[parents[to]]
            moved.append(links(ts.at[g, i], t.at[k, col], (row, to)))
        t[k, col] = rq[parents[col]]
        shared = [links(t.at[k, col], t.at[k, col], partner)]
        yield
        for i, (copy, (dz, dy)) in enumerate(zip(moved, offsets)):
            copy.wait_recv()
            got = t.at[k, plane(4 - dz, 4 - dy)]
            shared.append(links(got, got, partner))
            if i % 5 == 4:
                yield
        for copy in shared:
            copy.wait_recv()
        slots = u.shape[2]

        def parent_block(v):
            m = jnp.maximum(v - 128, 0)
            return t[lax.div(m, 32), lax.div(lax.rem(m, 32), 2), lax.rem(m, 2)]

        moved = []
        for d in (2, 1, 3):
            q = ring(x, d)
            for i in range(slots):
                u[g, d - 1, i] = parent_block(bl[col, (2 * q + k) * slots + i])
            moved.append(links(u.at[g, d - 1], bb.at[g, x], (2 * q + k, col)))
        for i in range(slots):
            bb[g, x, i] = parent_block(bl[col, row * slots + i])
        links.sent(used)
        yield
        for copy in moved:
            copy.wait_recv()
        for i in range(slots):
            v = bl[col, row * slots + i]
            side = root_block(jnp.minimum(v, 127)).astype(F32)
            for q in range(4):
                span = slice(q * quarter, (q + 1) * quarter)
                bound[g, span, i * BLOCK : (i + 1) * BLOCK] = jnp.where(
                    v < 128, side[span, :], bb[g, q, i].astype(F32)
                ).astype(BF)

        up, down = along["x"](1), along["x"](3)
        length = shift.shape[2]

        def scatter(product, rp, base, rf, rn):
            out = {}

            def make(d):
                q = ring(x, d)
                sp[g, d] = product(q, 1 - k).astype(BF)
                out[d] = links(sp.at[g, d], rp.at[g, d], partner)
                pool[g, d] = product(q, k)

            def prepare(d):
                if d == 2:
                    make(2)
                    make(1)
                    yield
                elif d == 1:
                    make(3)
                    yield
                elif d == 3:
                    make(0)
                out[d].wait_recv()

            def value(d, h):
                span = slice(h * tall, (h + 1) * tall)
                return pool[g, d, span, :] + rp[g, d, span, :].astype(F32)

            halves, used = yield from ring_sum(
                links, value, prepare, up, down,
                lambda i, h: sa.at[g, i, h, base : base + tall], rf.at[g], rn.at[g], None,
            )
            return halves, list(out.values())

        loaded("cl")
        halves, used = yield from scatter(
            lambda q, core: jnp.dot(
                bound[g],
                cl[:, pl.ds(pl.multiple_of((2 * q + core) * length, length), length)],
                preferred_element_type=F32,
            ),
            rp1, 0, rf1l, rn1l,
        )
        for h in range(2):
            shift[g, h * tall : (h + 1) * tall, :] = (
                leaf_t[lo + h * tall : lo + (h + 1) * tall, :].astype(F32) - halves[h]
            ).astype(BF)
        links.sent(used)
        loaded("dl")
        halves, used = yield from scatter(
            lambda q, core: lax.dot_general(
                shift[g],
                w[
                    pl.ds(pl.multiple_of((2 * lax.rem(q, 2) + core) * length, length), length),
                    pl.ds(pl.multiple_of(lax.div(q, 2) * length, length), length),
                ],
                NT,
                preferred_element_type=F32,
            ),
            rp2, tall, rf2l, rn2l,
        )
        for h in range(2):
            out_leaf[lo + h * tall : lo + (h + 1) * tall, :] = halves[h].astype(BF)

    together([program(g) for g in range(groups)], lag)
    links.drain()
    assert len(links.made) == send.shape[0], len(links.made)


def turned(*refs):
    half = len(refs) // 2
    for source, target in zip(refs[:half], refs[half:]):
        target[...] = source[...].T


VM = pl.BlockSpec(memory_space=pltpu.VMEM)
SM = pl.BlockSpec(memory_space=pltpu.SMEM)
ANY = pl.BlockSpec(memory_space=pl.ANY)
GROUPS = 2
COPIES = 124
LAG = 0


def shards(
    dinv_root, rhs_root, dinv_mid, coup_mid, rhs_mid, dinv_leaf, coup_leaf, rhs_leaf,
    bounds_mid, bounds_leaf, parents,
):
    n = rhs_root.shape[1]
    slots = bounds_leaf.shape[1] // 8
    wide = 2 * BLOCK
    length = rhs_leaf.shape[1]
    g, r = GROUPS, n // GROUPS
    scratch = [
        (rhs_root.shape, BF), (rhs_root.shape[::-1], BF),
        (rhs_mid.shape[1:], BF), ((n, length), BF), (rhs_leaf.shape[1:], BF), ((n, length), BF),
        (dinv_root.shape, BF), (coup_mid.shape, BF), (dinv_mid.shape, BF), (coup_leaf.shape[1:], BF),
        ((4, 2, 4, 4, r, BLOCK), BF), ((4, 2, 4, 4, r, BLOCK), BF),
        ((g, 4, r, length), F32), ((g, 4, r, wide), F32),
        ((g, 3, 2, r, length), BF), ((g, 3, r, wide), BF),
        ((g, 2, r, wide), BF), ((g, 2, 2, r, wide), BF),
        ((g, 3, r, BLOCK), BF),
        ((g, 2, r, length), BF), ((g, 2, 2, r, length), BF),
        ((g, 3, r, wide), BF),
        ((g, r, length), F32), ((g, r, length), BF),
        ((g, 4, 2, r // 4, BLOCK), BF), ((4, 2, r // 4, BLOCK), BF), ((4, 2, r // 4, BLOCK), BF),
        ((g, 15, 2, r // 4, BLOCK), BF), ((2, 16, 2, r // 4, BLOCK), BF), ((2, 16, 2, r // 4, BLOCK), BF),
        ((g, 3, slots, r // 4, BLOCK), BF), ((g, 4, slots, r // 4, BLOCK), BF),
        ((g, r, slots * BLOCK), BF),
        ((g, 4, r, length), BF), ((g, 4, r, length), BF), ((g, 4, r, length), BF),
        ((g, 2, r // 2, length), BF), ((g, 2, 2, r // 2, length), BF),
        ((g, 2, r // 2, length), BF), ((g, 2, 2, r // 2, length), BF),
    ]
    copies = COPIES * g
    outs = pl.pallas_call(
        functools.partial(kernel, GROUPS, LAG),
        out_shape=tuple(jax.ShapeDtypeStruct((n, width), BF) for width in (BLOCK, wide, length)),
        in_specs=[SM] * 3 + [ANY] * 8,
        out_specs=(VM,) * 3,
        scratch_shapes=[pltpu.VMEM(shape, kind) for shape, kind in scratch]
        + [
            pltpu.SemaphoreType.DMA((24,)),
            pltpu.SemaphoreType.DMA((copies,)),
            pltpu.SemaphoreType.DMA((copies,)),
        ],
        compiler_params=pltpu.CompilerParams(
            collective_id=0, has_side_effects=True, vmem_limit_bytes=67043328
        ),
    )(
        bounds_mid, bounds_leaf, parents, rhs_root, rhs_mid, rhs_leaf[0],
        dinv_root, coup_mid, dinv_mid, coup_leaf[0], dinv_leaf[0],
    )
    root, mid, leaf = pl.pallas_call(
        turned,
        out_shape=tuple(jax.ShapeDtypeStruct(out.shape[::-1], BF) for out in outs),
        in_specs=[VM] * 3,
        out_specs=(VM,) * 3,
    )(*outs)
    return root, mid, leaf[None]


def solution(mesh):
    return jax.shard_map(
        shards,
        mesh=mesh,
        in_specs=(
            P("row", "col"),
            P("col", None),
            P("row", "col"),
            P("row", "col"),
            P(None, "col", None),
            P("col", None, "row"),
            P("col", "row", None),
            P("col", "row", None),
            P(),
            P(),
            P(),
        ),
        out_specs=(P(("row", "col"), None), P(("row", "col"), None), P("col", "row", None)),
        check_vma=False,
    )
```

time: 577 us -> 148 us (0.26)
  waiting for transfers between devices: 387 us -> 0 us
  Pallas kernels: 0 us -> 147 us
  local copies, waits for them, and re-layouts: 72.1 us -> 0 us
  matrix products: 44.2 us -> 0 us
  blocking collectives: 40.3 us -> 0 us
  between operations: 15.6 us -> 0.64 us
  starting transfers between devices: 8.16 us -> 0 us
  other arithmetic: 7.39 us -> 0 us
    reduce_scatter x4 -> x0, waiting for transfers between devices: 239 us -> none  [the longest x1 79.4 us: shards(): lax.psum_scatter(jnp.dot(dinv_mid, shift_mid, preferred_element_type=jnp....]
    pallas_call x0 -> x2, Pallas kernels: none -> 147 us  [the longest x1 145 us: shards(): pl.pallas_call(functools.partial(kernel, GROUPS, LAG), out_shape=tuple((j...]
    all_gather x2 -> x0, waiting for transfers between devices: 125 us -> none  [the longest x1 74.7 us: shards(): lax.all_gather(root_values, ('row', 'col'), axis=0, tiled=True)]
    dot_general x7 -> x0, matrix products: 44.2 us -> none  [the longest x2 13 us: transposed_product(): lax.dot_general(coupling, boundary, (((0,), (0,)), ((), ())), preferred_e...]
    unnamed x1 -> x0, blocking collectives: 40.3 us -> none
    unnamed x21 -> x0, local copies, waits for them, and re-layouts: 36.2 us -> none
    reshape x2 -> x0, local copies, waits for them, and re-layouts: 21.3 us -> none  [the longest x1 16.4 us: pick_blocks(): flat_blocks = shard_rows.reshape(block_count, BLOCK * shard_rows.shape[1])]
    unnamed x8 -> x0, waiting for transfers between devices: 21.2 us -> none
  transfers between devices with their start and end apart: 9 -> 0, of which waited for: 8 -> 0; matrix products, arithmetic and copies ran while one was open for 1% -> 0% of each run, Pallas kernels for 0% -> 0%
where the time goes in v2:
time: 148 us
  Pallas kernels  147 us (99%)
    pallas_call x1, Pallas kernels, shards(): pl.pallas_call(functools.partial(kernel, GROUPS, LAG), out_shape=tuple((j...  145 us

profile of v2, /device:TPU:1, one launch (start us, length us, event | category | flops | bytes accessed | tf_op | source)
XLA Modules:
  0.0 147.8 jit_solution(1730317345992808307)
XLA Ops:
  0.6 145.1 %shard_map.130 = (bf16[384,128]{1,0:T(8,128)(2,1)}, bf16[384,256]{1,0:T(8,128)(2,1)}, bf16[384,512]{1,0:T(8,128)(2,1)}) custom-call(s32[4,64]{1,0:T(4,128)} %bm.1, s32[16,48]{1,0:T(8,128)} %bl.1, s32[16]{0:T(128)} %parents.1, bf16[1024,384]{1,0:T(8,128)(2,1)} %root_hbm.1, bf16[4,512,384]{2,1,0:T(8,128)(2,1)} %mid_hbm.1, bf16[512,384]{1,0:T(8,128)(2,1)} %bitcast.6, ...), custom_call_target="tpu_custom_call" | custom-call | tf_op jit(solution)/shard_map/pallas_call | solution.py:529
  145.7 2.1 %shard_map.131 = (bf16[128,384]{1,0:T(8,128)(2,1)}, bf16[256,384]{1,0:T(8,128)(2,1)}, bf16[512,384]{1,0:T(8,128)(2,1)}) custom-call(bf16[384,128]{1,0:T(8,128)(2,1)} %get-tuple-element.9.refs_0_, bf16[384,256]{1,0:T(8,128)(2,1)} %get-tuple-element.10.refs_1_, bf16[384,512]{1,0:T(8,128)(2,1)} %get-tuple-element.11.refs_2_), custom_call_target="tpu_custom_call" | custom-call | tf_op jit(solution)/shard_map/pallas_call | solution.py:547

commit v3 on v2

--- a/solution.py
+++ b/solution.py
@@ -51,23 +51,25 @@
         self.sent(self.made)
 
 
-def greet(peers):
+def greet(peers, meanwhile):
     barrier = pltpu.get_barrier_semaphore()
     for peer in peers:
         pl.semaphore_signal(barrier, inc=1, device_id=peer, device_id_type=MESH)
+    meanwhile()
     pl.semaphore_wait(barrier, len(peers))
 
 
 def ring_sum(links, value, prepare, up, down, s, rf, rn, p):
-    yield from prepare(2)
+    prepare(2)
     s(1, 0)[...] = value(2, 0).astype(BF)
     far_up = links(s(1, 0), rf.at[0], up)
     s(1, 1)[...] = value(2, 1).astype(BF)
     far_down = links(s(1, 1), rf.at[1], down)
-    yield from prepare(1)
+    yield
+    prepare(1)
     s(0, 1)[...] = value(1, 1).astype(BF)
     last = [links(s(0, 1), rn.at[0, 1], up)]
-    yield from prepare(3)
+    prepare(3)
     s(2, 0)[...] = value(3, 0).astype(BF)
     last.append(links(s(2, 0), rn.at[1, 0], down))
     if p is not None:
@@ -82,7 +84,7 @@
     far_down.wait_recv()
     s(2, 1)[...] = (kept(1, 3, 1) + rf[1].astype(F32)).astype(BF)
     last.append(links(s(2, 1), rn.at[1, 1], down))
-    yield from prepare(0)
+    prepare(0)
     yield
     for copy in last:
         copy.wait_recv()
@@ -106,8 +108,7 @@
 
 
 def nothing(d):
-    return
-    yield
+    pass
 
 
 def together(programs, lag):
@@ -165,16 +166,19 @@
     here = {"x": x, "y": y, "z": z}
     first_ring = (row, chip(ring(a, 1), b)), (row, chip(ring(a, 3), b))
     second_ring = lambda d: (row, chip(a, ring(b, d)))
-    greet(
-        [(row, plane(*o)) for o in offsets] + [along["x"](d) for d in (1, 2, 3)] + [partner]
-    )
-    links = Links(send, recv)
     def loaded(name):
         for copy in loads.pop(name, ()):
             copy.wait()
 
-    loaded("root")
-    root_t[...] = root_v[...].T
+    def turn_root():
+        loaded("root")
+        root_t[...] = root_v[...].T
+
+    greet(
+        [(row, plane(*o)) for o in offsets] + [along["x"](d) for d in (1, 2, 3)] + [partner],
+        turn_root,
+    )
+    links = Links(send, recv)
     passed = []
 
     def root_done():
@@ -378,12 +382,10 @@
         t[k, col] = rq[parents[col]]
         shared = [links(t.at[k, col], t.at[k, col], partner)]
         yield
-        for i, (copy, (dz, dy)) in enumerate(zip(moved, offsets)):
+        for copy, (dz, dy) in zip(moved, offsets):
             copy.wait_recv()
             got = t.at[k, plane(4 - dz, 4 - dy)]
             shared.append(links(got, got, partner))
-            if i % 5 == 4:
-                yield
         for copy in shared:
             copy.wait_recv()
         slots = u.shape[2]
@@ -429,10 +431,8 @@
                 if d == 2:
                     make(2)
                     make(1)
-                    yield
                 elif d == 1:
                     make(3)
-                    yield
                 elif d == 3:
                     make(0)
                 out[d].wait_recv()

time: 148 us -> 136 us (0.919)
  Pallas kernels: 147 us -> 135 us
    pallas_call x1, Pallas kernels: 145 us -> 133 us  [shards(): pl.pallas_call(functools.partial(kernel, GROUPS, LAG), out_shape=tuple((j...]
where the time goes in v3:
time: 136 us; the launch traced here: 135 us
  Pallas kernels  135 us (99%)
    pallas_call x1, Pallas kernels, shards(): pl.pallas_call(functools.partial(kernel, GROUPS, LAG), out_shape=tuple((j...  133 us

profile of v3, /device:TPU:1, one launch (start us, length us, event | category | flops | bytes accessed | tf_op | source)
XLA Modules:
  0.0 135.4 jit_solution(11775894638174380592)
XLA Ops:
  0.6 132.6 %shard_map.130 = (bf16[384,128]{1,0:T(8,128)(2,1)}, bf16[384,256]{1,0:T(8,128)(2,1)}, bf16[384,512]{1,0:T(8,128)(2,1)}) custom-call(s32[4,64]{1,0:T(4,128)} %bm.1, s32[16,48]{1,0:T(8,128)} %bl.1, s32[16]{0:T(128)} %parents.1, bf16[1024,384]{1,0:T(8,128)(2,1)} %root_hbm.1, bf16[4,512,384]{2,1,0:T(8,128)(2,1)} %mid_hbm.1, bf16[512,384]{1,0:T(8,128)(2,1)} %bitcast.6, ...), custom_call_target="tpu_custom_call" | custom-call | tf_op jit(solution)/shard_map/pallas_call | solution.py:529
  133.2 2.1 %shard_map.131 = (bf16[128,384]{1,0:T(8,128)(2,1)}, bf16[256,384]{1,0:T(8,128)(2,1)}, bf16[512,384]{1,0:T(8,128)(2,1)}) custom-call(bf16[384,128]{1,0:T(8,128)(2,1)} %get-tuple-element.9.refs_0_, bf16[384,256]{1,0:T(8,128)(2,1)} %get-tuple-element.10.refs_1_, bf16[384,512]{1,0:T(8,128)(2,1)} %get-tuple-element.11.refs_2_), custom_call_target="tpu_custom_call" | custom-call | tf_op jit(solution)/shard_map/pallas_call | solution.py:547

commit v4 on v3

--- a/solution.py
+++ b/solution.py
@@ -73,18 +73,20 @@
     s(2, 0)[...] = value(3, 0).astype(BF)
     last.append(links(s(2, 0), rn.at[1, 0], down))
     if p is not None:
-        for i, term in enumerate(((1, 0), (3, 1), (0, 0), (0, 1))):
+        for i, term in enumerate(((1, 0), (3, 1))):
             p(i)[...] = value(*term)
     kept = (lambda i, d, h: p(i)[...]) if p is not None else (lambda i, d, h: value(d, h))
     yield
     far_up.wait_recv()
     s(0, 0)[...] = (kept(0, 1, 0) + rf[0].astype(F32)).astype(BF)
     last.append(links(s(0, 0), rn.at[0, 0], up))
-    yield
     far_down.wait_recv()
     s(2, 1)[...] = (kept(1, 3, 1) + rf[1].astype(F32)).astype(BF)
     last.append(links(s(2, 1), rn.at[1, 1], down))
     prepare(0)
+    if p is not None:
+        for i, term in enumerate(((0, 0), (0, 1))):
+            p(2 + i)[...] = value(*term)
     yield
     for copy in last:
         copy.wait_recv()
@@ -289,8 +291,9 @@
                 own = piece(part, 0)
                 axis = order[phase]
                 state.append((links(own, own, along[axis](1)), links(own, own, along[axis](3))))
-                if phase == 2:
-                    share(own)
+            if phase == 2:
+                for part in range(len(orders)):
+                    share(piece(part, 0))
             yield
             onward = []
             for part, order in enumerate(orders):
@@ -301,7 +304,8 @@
                 state[part][1].wait_recv()
                 got = piece(part, 1, 1)
                 onward.append((first, links(got, got, along[axis](3))))
-                if phase == 2:
+            if phase == 2:
+                for part in range(len(orders)):
                     share(piece(part, 3))
                     share(piece(part, 1))
             yield

time: 136 us -> 135 us (level)
  no operation moved by 1% of the time
where the time goes in v4:
time: 135 us
  Pallas kernels  134 us (99%)
    pallas_call x1, Pallas kernels, shards(): pl.pallas_call(functools.partial(kernel, GROUPS, LAG), out_shape=tuple((j...  132 us

profile of v4, /device:TPU:1, one launch (start us, length us, event | category | flops | bytes accessed | tf_op | source)
XLA Modules:
  0.0 134.5 jit_solution(3992893294491118976)
XLA Ops:
  0.6 131.7 %shard_map.130 = (bf16[384,128]{1,0:T(8,128)(2,1)}, bf16[384,256]{1,0:T(8,128)(2,1)}, bf16[384,512]{1,0:T(8,128)(2,1)}) custom-call(s32[4,64]{1,0:T(4,128)} %bm.1, s32[16,48]{1,0:T(8,128)} %bl.1, s32[16]{0:T(128)} %parents.1, bf16[1024,384]{1,0:T(8,128)(2,1)} %root_hbm.1, bf16[4,512,384]{2,1,0:T(8,128)(2,1)} %mid_hbm.1, bf16[512,384]{1,0:T(8,128)(2,1)} %bitcast.6, ...), custom_call_target="tpu_custom_call" | custom-call | tf_op jit(solution)/shard_map/pallas_call | solution.py:533
  132.4 2.1 %shard_map.131 = (bf16[128,384]{1,0:T(8,128)(2,1)}, bf16[256,384]{1,0:T(8,128)(2,1)}, bf16[512,384]{1,0:T(8,128)(2,1)}) custom-call(bf16[384,128]{1,0:T(8,128)(2,1)} %get-tuple-element.9.refs_0_, bf16[384,256]{1,0:T(8,128)(2,1)} %get-tuple-element.10.refs_1_, bf16[384,512]{1,0:T(8,128)(2,1)} %get-tuple-element.11.refs_2_), custom_call_target="tpu_custom_call" | custom-call | tf_op jit(solution)/shard_map/pallas_call | solution.py:551
